TPU v7x, 32 devices: a whole 2x2x4 slice. The times are simulated.
32 devices in a mesh: dp: 4 (over x, core), seq: 8 (over z, y).
Axes of the slice: x: 2, y: 2, z: 4, core: 2. Of those that a mesh axis runs over, the one named last changes fastest.
Arguments:
- patches: bfloat16 [4, 4096, 6144], P('dp', 'seq'), may hold values from -6 to 6
- embedding: bfloat16 [6144, 768], P('seq'), may hold values from -0.078125 to 0.078125
- first_gain: bfloat16 [768], P('seq'), may hold values from 0.5 to 1.5
- first_shift: bfloat16 [768], P('seq'), may hold values from -4 to 4
- joint_weight: bfloat16 [768, 2304], P('seq'), may hold values from -0.3125 to 0.3125
- output_weight: bfloat16 [768, 768], P('seq'), may hold values from -0.875 to 0.875
- second_gain: bfloat16 [768], P('seq'), may hold values from 0.5 to 1.5
- second_shift: bfloat16 [768], P('seq'), may hold values from -4 to 4
- up_weight: bfloat16 [768, 3072], P('seq'), may hold values from -0.21875 to 0.21875
- up_bias: bfloat16 [3072], P('seq'), may hold values from -6 to 6
- down_weight: bfloat16 [3072, 768], P('seq'), may hold values from -0.109375 to 0.109375
- down_bias: bfloat16 [768], P('seq'), may hold values from -6 to 6
- block_number: int32 [4, 4096], P('dp'), may hold values from 0 to 31, never falling along the last dimension, each value on 1 to 256 neighbouring positions
- cotangent: bfloat16 [4, 4096, 768], P('dp', 'seq'), may hold values from -6 to 6
Outputs:
- block_output: bfloat16 [4, 4096, 768], P('dp', 'seq')
- patches_gradient: bfloat16 [4, 4096, 6144], P('dp', 'seq')
- embedding_gradient: float32 [6144, 768], P('seq')
- first_gain_gradient: float32 [768], P('seq')
- first_shift_gradient: float32 [768], P('seq')
- joint_weight_gradient: float32 [768, 2304], P('seq')
- output_weight_gradient: float32 [768, 768], P('seq')
- second_gain_gradient: float32 [768], P('seq')
- second_shift_gradient: float32 [768], P('seq')
- up_weight_gradient: float32 [768, 3072], P('seq')
- up_bias_gradient: float32 [3072], P('seq')
- down_weight_gradient: float32 [3072, 768], P('seq')
- down_bias_gradient: float32 [768], P('seq')
Inputs may be any that keep to these rules, and one draw needn't show every extreme that they name: `block_number`: in each sequence the block numbers never fall along the rows; each block has 1 to 256 rows, and some block has exactly 256.
All inputs are finite; a program needn't handle non-finite values.
Results may differ from a plain program's by a relative error of at most 0.038.
Values may be sent and summed in bfloat16 or wider, within the bound.
No kernel may reach another device: no remote copies, remote signals or barrier semaphores. Data moves between devices by JAX's collectives and lax.ppermute only.
A program may use at most 256 MiB of HBM per device.

v0:
```python
import math
import jax
import jax.numpy as jnp
from jax import lax
from jax.sharding import PartitionSpec as P

HEADS = 12
HEAD_DIM = 64
EPS = 1e-05
NEG = -1e30


def layer_norm(values, gain, shift):
    center = values - jnp.mean(values, axis=-1, keepdims=True)
    spread = jnp.mean(center * center, axis=-1, keepdims=True)
    return center * lax.rsqrt(spread + EPS) * gain + shift


def gelu_tanh(values):
    return jax.nn.gelu(values, approximate=True)


def masked_scores(query, keys, query_ids, key_ids, scale):
    scores = jnp.einsum("sqhd,skhd->shqk", query, keys, preferred_element_type=jnp.float32) * scale
    visible = key_ids[:, None, None, :] <= query_ids[:, None, :, None]
    return jnp.where(visible, scores, NEG)


def per_device(
    patches,
    embedding,
    first_gain,
    first_shift,
    joint_weight,
    output_weight,
    second_gain,
    second_shift,
    up_weight,
    up_bias,
    down_weight,
    down_bias,
    block_number,
    cotangent,
):
    seqs_here, rows_here, width_in = patches.shape
    model = HEADS * HEAD_DIM
    count_rows = seqs_here * rows_here
    length = block_number.shape[1]
    scale = HEAD_DIM ** (-0.5)
    gathered_params = (
        lax.all_gather(embedding, "seq", axis=0, tiled=True),
        lax.all_gather(first_gain, "seq", axis=0, tiled=True),
        lax.all_gather(first_shift, "seq", axis=0, tiled=True),
        lax.all_gather(joint_weight, "seq", axis=0, tiled=True),
        lax.all_gather(output_weight, "seq", axis=0, tiled=True),
        lax.all_gather(second_gain, "seq", axis=0, tiled=True),
        lax.all_gather(second_shift, "seq", axis=0, tiled=True),
        lax.all_gather(up_weight, "seq", axis=0, tiled=True),
        lax.all_gather(up_bias, "seq", axis=0, tiled=True),
        lax.all_gather(down_weight, "seq", axis=0, tiled=True),
        lax.all_gather(down_bias, "seq", axis=0, tiled=True),
    )
    (
        embed_full,
        gain_one,
        shift_one,
        joint_full,
        output_full,
        gain_two,
        shift_two,
        up_full,
        upbias_full,
        down_full,
        downbias_full,
    ) = gathered_params
    flat_in = patches.reshape(count_rows, width_in)
    hidden = jnp.dot(flat_in, embed_full, preferred_element_type=jnp.float32)
    normed1 = layer_norm(
        hidden, gain_one.astype(jnp.float32), shift_one.astype(jnp.float32)
    ).astype(jnp.bfloat16)
    joint = jnp.dot(normed1, joint_full, preferred_element_type=jnp.float32).astype(jnp.bfloat16)
    query = joint[:, :model].reshape(seqs_here, rows_here, HEADS, HEAD_DIM)
    local_pairs = joint[:, model:].reshape(seqs_here, rows_here, 2 * model)
    sequence_pairs = lax.all_gather(local_pairs, "seq", axis=1, tiled=True)
    keys_all = sequence_pairs[:, :, :model].reshape(seqs_here, length, HEADS, HEAD_DIM)
    values_all = sequence_pairs[:, :, model:].reshape(seqs_here, length, HEADS, HEAD_DIM)
    offset = lax.axis_index("seq") * rows_here
    query_ids = lax.dynamic_slice_in_dim(block_number, offset, rows_here, 1)
    last_ids = query_ids[:, -1]
    reach = jnp.max(jnp.sum((block_number <= last_ids[:, None]).astype(jnp.int32), axis=1))
    key_width = math.gcd(length, 512)
    starts = jnp.arange(length // key_width, dtype=jnp.int32) * key_width

    def key_slice(start, width):
        keys = lax.dynamic_slice_in_dim(keys_all, start, width, 1)
        values = lax.dynamic_slice_in_dim(values_all, start, width, 1)
        key_ids = lax.dynamic_slice_in_dim(block_number, start, width, 1)
        return (keys, values, key_ids)

    def total_step(carry, start):

        def total_visit(state):
            top, total = state
            keys, values, key_ids = key_slice(start, key_width)
            scores = masked_scores(query, keys, query_ids, key_ids, scale)
            new_top = jnp.maximum(top, jnp.max(scores, axis=-1))
            total = total * jnp.exp(top - new_top) + jnp.sum(
                jnp.exp(scores - new_top[..., None]), axis=-1
            )
            return (new_top, total)

        return (lax.cond(start < reach, total_visit, lambda state: state, carry), None)

    start_top = jnp.full((seqs_here, HEADS, rows_here), NEG, jnp.float32)
    start_total = jnp.zeros((seqs_here, HEADS, rows_here), jnp.float32)
    (top, total), _ = lax.scan(total_step, (start_top, start_total), starts)
    log_total = top + jnp.log(total)

    def output_step(accum, start):

        def output_visit(acc):
            keys, values, key_ids = key_slice(start, key_width)
            probs = jnp.exp(
                masked_scores(query, keys, query_ids, key_ids, scale) - log_total[..., None]
            ).astype(jnp.bfloat16)
            return acc + jnp.einsum(
                "shqk,skhd->sqhd", probs, values, preferred_element_type=jnp.float32
            )

        return (lax.cond(start < reach, output_visit, lambda acc: acc, accum), None)

    zero_query = jnp.zeros((seqs_here, rows_here, HEADS, HEAD_DIM), jnp.float32)
    attended, _ = lax.scan(output_step, zero_query, starts)
    attended_low = attended.reshape(count_rows, model).astype(jnp.bfloat16)
    resid = hidden + jnp.dot(attended_low, output_full, preferred_element_type=jnp.float32)
    gain_second = gain_two.astype(jnp.float32)
    shift_second = shift_two.astype(jnp.float32)
    normed2 = layer_norm(resid, gain_second, shift_second).astype(jnp.bfloat16)
    upper = jnp.dot(normed2, up_full, preferred_element_type=jnp.float32) + upbias_full.astype(
        jnp.float32
    )
    gate = gelu_tanh(upper).astype(jnp.bfloat16)
    lowered = jnp.dot(gate, down_full, preferred_element_type=jnp.float32) + downbias_full.astype(
        jnp.float32
    )
    block_output = (resid + lowered).astype(jnp.bfloat16).reshape(seqs_here, rows_here, model)
    again_params = (
        lax.all_gather(embedding, "seq", axis=0, tiled=True),
        lax.all_gather(first_gain, "seq", axis=0, tiled=True),
        lax.all_gather(first_shift, "seq", axis=0, tiled=True),
        lax.all_gather(joint_weight, "seq", axis=0, tiled=True),
        lax.all_gather(output_weight, "seq", axis=0, tiled=True),
        lax.all_gather(second_gain, "seq", axis=0, tiled=True),
        lax.all_gather(second_shift, "seq", axis=0, tiled=True),
        lax.all_gather(up_weight, "seq", axis=0, tiled=True),
        lax.all_gather(up_bias, "seq", axis=0, tiled=True),
        lax.all_gather(down_weight, "seq", axis=0, tiled=True),
        lax.all_gather(down_bias, "seq", axis=0, tiled=True),
    )
    (
        embed_back,
        gain_one_back,
        shift_one_back,
        joint_back,
        output_back,
        gain_two_back,
        shift_two_back,
        up_back,
        upbias_back,
        down_back,
        downbias_back,
    ) = again_params
    tangent = cotangent.reshape(count_rows, model)
    down_bias_grad = jnp.sum(tangent.astype(jnp.float32), axis=0)
    down_weight_grad = jnp.dot(gate.T, tangent, preferred_element_type=jnp.float32)
    gate_grad = jnp.dot(tangent, down_back.T, preferred_element_type=jnp.float32)
    _, gelu_pull = jax.vjp(gelu_tanh, upper)
    upper_grad = gelu_pull(gate_grad)[0].astype(jnp.bfloat16)
    up_bias_grad = jnp.sum(upper_grad.astype(jnp.float32), axis=0)
    up_weight_grad = jnp.dot(normed2.T, upper_grad, preferred_element_type=jnp.float32)
    normed2_grad = jnp.dot(upper_grad, up_back.T, preferred_element_type=jnp.float32)
    _, second_pull = jax.vjp(
        layer_norm, resid, gain_two_back.astype(jnp.float32), shift_two_back.astype(jnp.float32)
    )
    resid_part, second_gain_grad, second_shift_grad = second_pull(normed2_grad)
    resid_grad = tangent.astype(jnp.float32) + resid_part
    mixed_grad = resid_grad.astype(jnp.bfloat16)
    output_weight_grad = jnp.dot(attended_low.T, mixed_grad, preferred_element_type=jnp.float32)
    attended_grad = jnp.dot(mixed_grad, output_back.T, preferred_element_type=jnp.float32).astype(
        jnp.bfloat16
    )
    attended_grad = attended_grad.reshape(seqs_here, rows_here, HEADS, HEAD_DIM)
    delta = jnp.transpose(jnp.sum(attended_grad.astype(jnp.float32) * attended, axis=-1), (0, 2, 1))

    def score_pieces(start, width):
        keys, values, key_ids = key_slice(start, width)
        probs = jnp.exp(
            masked_scores(query, keys, query_ids, key_ids, scale) - log_total[..., None]
        )
        prob_grad = jnp.einsum(
            "sqhd,skhd->shqk", attended_grad, values, preferred_element_type=jnp.float32
        )
        score_grad = (probs * (prob_grad - delta[..., None])).astype(jnp.bfloat16)
        return (keys, probs, score_grad)

    def query_from(keys, score_grad):
        return (
            jnp.einsum("shqk,skhd->sqhd", score_grad, keys, preferred_element_type=jnp.float32)
            * scale
        )

    def pair_from(probs, score_grad, width):
        rounded = probs.astype(jnp.bfloat16)
        value_grad = jnp.einsum(
            "shqk,sqhd->skhd", rounded, attended_grad, preferred_element_type=jnp.float32
        )
        key_grad = (
            jnp.einsum("shqk,sqhd->skhd", score_grad, query, preferred_element_type=jnp.float32)
            * scale
        )
        paired = jnp.concatenate(
            [
                key_grad.reshape(seqs_here, width, model),
                value_grad.reshape(seqs_here, width, model),
            ],
            axis=-1,
        )
        return jnp.transpose(paired, (1, 0, 2))

    def both_grads(start, width):
        keys, probs, score_grad = score_pieces(start, width)
        return (query_from(keys, score_grad), pair_from(probs, score_grad, width))

    def whole_step(accum, start):
        empty_pair = jnp.zeros((key_width, seqs_here, 2 * model), jnp.float32)
        query_part, paired = lax.cond(
            start < reach, lambda: both_grads(start, key_width), lambda: (zero_query, empty_pair)
        )
        return (accum + query_part, paired)

    query_total, stacked = lax.scan(whole_step, zero_query, starts)
    every_pair = stacked.reshape(length, seqs_here, 2 * model)
    own_pairs = lax.psum_scatter(
        every_pair.astype(jnp.bfloat16), "seq", scatter_dimension=0, tiled=True
    ).astype(jnp.float32)
    pair_local = jnp.transpose(own_pairs, (1, 0, 2)).reshape(count_rows, 2 * model)
    joint_grad = jnp.concatenate(
        [query_total.reshape(count_rows, model), pair_local], axis=-1
    ).astype(jnp.bfloat16)
    joint_weight_grad = jnp.dot(normed1.T, joint_grad, preferred_element_type=jnp.float32)
    normed1_grad = jnp.dot(joint_grad, joint_back.T, preferred_element_type=jnp.float32)
    _, first_pull = jax.vjp(
        layer_norm, hidden, gain_one_back.astype(jnp.float32), shift_one_back.astype(jnp.float32)
    )
    hidden_part, first_gain_grad, first_shift_grad = first_pull(normed1_grad)
    hidden_grad = (resid_grad + hidden_part).astype(jnp.bfloat16)
    embedding_grad = jnp.dot(flat_in.T, hidden_grad, preferred_element_type=jnp.float32)
    patches_grad = jnp.dot(hidden_grad, embed_back.T, preferred_element_type=jnp.float32).astype(
        jnp.bfloat16
    )
    patches_grad = patches_grad.reshape(seqs_here, rows_here, width_in)
    group_terms = (
        lax.psum_scatter(
            embedding_grad.astype(jnp.bfloat16), "seq", scatter_dimension=0, tiled=True
        ).astype(jnp.float32),
        lax.psum_scatter(
            first_gain_grad.astype(jnp.bfloat16), "seq", scatter_dimension=0, tiled=True
        ).astype(jnp.float32),
        lax.psum_scatter(
            first_shift_grad.astype(jnp.bfloat16), "seq", scatter_dimension=0, tiled=True
        ).astype(jnp.float32),
        lax.psum_scatter(
            joint_weight_grad.astype(jnp.bfloat16), "seq", scatter_dimension=0, tiled=True
        ).astype(jnp.float32),
        lax.psum_scatter(
            output_weight_grad.astype(jnp.bfloat16), "seq", scatter_dimension=0, tiled=True
        ).astype(jnp.float32),
        lax.psum_scatter(
            second_gain_grad.astype(jnp.bfloat16), "seq", scatter_dimension=0, tiled=True
        ).astype(jnp.float32),
        lax.psum_scatter(
            second_shift_grad.astype(jnp.bfloat16), "seq", scatter_dimension=0, tiled=True
        ).astype(jnp.float32),
        lax.psum_scatter(
            up_weight_grad.astype(jnp.bfloat16), "seq", scatter_dimension=0, tiled=True
        ).astype(jnp.float32),
        lax.psum_scatter(
            up_bias_grad.astype(jnp.bfloat16), "seq", scatter_dimension=0, tiled=True
        ).astype(jnp.float32),
        lax.psum_scatter(
            down_weight_grad.astype(jnp.bfloat16), "seq", scatter_dimension=0, tiled=True
        ).astype(jnp.float32),
        lax.psum_scatter(
            down_bias_grad.astype(jnp.bfloat16), "seq", scatter_dimension=0, tiled=True
        ).astype(jnp.float32),
    )
    totals = (
        lax.psum(group_terms[0].astype(jnp.bfloat16), "dp").astype(jnp.float32),
        lax.psum(group_terms[1].astype(jnp.bfloat16), "dp").astype(jnp.float32),
        lax.psum(group_terms[2].astype(jnp.bfloat16), "dp").astype(jnp.float32),
        lax.psum(group_terms[3].astype(jnp.bfloat16), "dp").astype(jnp.float32),
        lax.psum(group_terms[4].astype(jnp.bfloat16), "dp").astype(jnp.float32),
        lax.psum(group_terms[5].astype(jnp.bfloat16), "dp").astype(jnp.float32),
        lax.psum(group_terms[6].astype(jnp.bfloat16), "dp").astype(jnp.float32),
        lax.psum(group_terms[7].astype(jnp.bfloat16), "dp").astype(jnp.float32),
        lax.psum(group_terms[8].astype(jnp.bfloat16), "dp").astype(jnp.float32),
        lax.psum(group_terms[9].astype(jnp.bfloat16), "dp").astype(jnp.float32),
        lax.psum(group_terms[10].astype(jnp.bfloat16), "dp").astype(jnp.float32),
    )
    return (
        block_output,
        patches_grad,
        totals[0],
        totals[1],
        totals[2],
        totals[3],
        totals[4],
        totals[5],
        totals[6],
        totals[7],
        totals[8],
        totals[9],
        totals[10],
    )


def solution(mesh):
    placed = (
        P("dp", "seq", None),
        P("seq", None),
        P("seq"),
        P("seq"),
        P("seq", None),
        P("seq", None),
        P("seq"),
        P("seq"),
        P("seq", None),
        P("seq"),
        P("seq", None),
        P("seq"),
        P("dp", None),
        P("dp", "seq", None),
    )
    return jax.shard_map(
        per_device,
        mesh=mesh,
        in_specs=placed,
        out_specs=(
            P("dp", "seq", None),
            P("dp", "seq", None),
            P("seq", None),
            P("seq"),
            P("seq"),
            P("seq", None),
            P("seq", None),
            P("seq"),
            P("seq"),
            P("seq", None),
            P("seq"),
            P("seq", None),
            P("seq"),
        ),
        check_vma=False,
    )
```

profile of v0, /device:TPU:0, one launch (start us, length us, event | category | flops | bytes accessed | tf_op | source)
XLA Modules:
  0.0 1777.7 jit_solution(17283474801182536518)
XLA Ops:
  14.1 24.6 %all-reduce.12 = (bf16[768]{0:T(1024)(128)(2,1)S(1)}, bf16[768]{0:T(1024)(128)(2,1)S(1)}, bf16[768]{0:T(1024)(128)(2,1)S(1)}, bf16[768]{0:T(1024)(128)(2,1)S(1)}) all-reduce(bf16[768]{0:T(1024)(128)(2,1)S(1)} %dynamic-update-slice.1, bf16[768]{0:T(1024)(128)(2,1)S(1)} %dynamic-update-slice, ...), channel_id=1, replica_groups=mesh['dp'=4,'seq'=8] {'seq'}, use_global_device_ids=true, to_apply=%add.1 | all-reduce | flops 3072 | bytes 12288
  38.7 112.0 %all-gather.9.cloned.1.call-done = bf16[6144,768]{1,0:T(8,128)(2,1)} async-done(((bf16[768,768]{1,0:T(8,128)(2,1)}), bf16[6144,768]{1,0:T(8,128)(2,1)}) %all-gather.9.cloned.1.call-update) | async-done | bytes 9437200 | tf_op jit(solution)/shard_map/all_gather | solution.py:51
  150.7 9.7 fusion.81
  160.8 54.9 %all-gather.11.cloned.1.call-done = bf16[768,2304]{1,0:T(8,128)(2,1)} async-done(((bf16[96,2304]{1,0:T(8,128)(2,1)}), bf16[768,2304]{1,0:T(8,128)(2,1)}) %all-gather.11.cloned.1.call-update) | async-done | bytes 3538960 | tf_op jit(solution)/shard_map/all_gather | solution.py:54
  215.7 4.1 convolution_convert_fusion.5
  224.4 27.1 %all-gather.1 = bf16[8,1,384]{2,1,0:T(2,128)(2,1)S(1)} all-gather(bf16[1,1,384]{2,1,0:T(2,128)(2,1)S(1)} %reshape.385), channel_id=1, replica_groups=mesh['dp'=4,'seq'=8] {'seq'}, dimensions={0}, use_global_device_ids=true | all-gather | bytes 6912 | tf_op jit(solution)/shard_map/all_gather | solution.py:59
  254.6 143.0 %all-gather.19.cloned.1.call-done = bf16[4096,1536]{1,0:T(8,128)(2,1)} async-done(((bf16[512,1536]{1,0:T(8,128)(2,1)}), bf16[4096,1536]{1,0:T(8,128)(2,1)}) %all-gather.19.cloned.1.call-update) | async-done | bytes 12582928 | tf_op jit(solution)/shard_map/all_gather | solution.py:84
  397.6 10.2 fusion.79
  407.8 8.7 copy.68
  416.5 8.6 copy.67
  425.1 35.6 %while.38 = (s32[]{:T(128)}, f32[1,12,512]{2,1,0:T(8,128)S(1)}, f32[1,12,512]{2,1,0:T(8,128)S(1)}, s32[8]{0:T(128)S(1)}, s32[]{:T(128)}, /*index=5*/s32[1,4096]{...) while((s32[]{:T(128)}, f32[1,12,512]{2,1,0:T(8,128)S(1)}, ...), condition=%wide.region_8.0_spmd, body=%wide.region_3.8_spmd.sunk | while | flops 424947712 | bytes 27853072 | solution.py:116
  427.0 10.1 conditional.7
  429.3 5.2 fusion
  434.5 2.6 exponential_reduce_fusion
  439.0 10.1 conditional.7
  441.3 5.2 fusion
  446.6 2.6 exponential_reduce_fusion
  460.9 33.7 %while.39 = (s32[]{:T(128)}, f32[1,512,12,64]{1,3,2,0:T(8,128)S(1)}, s32[8]{0:T(128)S(1)}, s32[]{:T(128)}, bf16[1,4096,12,64]{1,3,2,0:T(8,128)(2,1)}, /*index=5*...) while((s32[]{:T(128)}, ...), condition=%wide.region_12.13_spmd, body=%wide.region_9.0_spmd.sunk | while | flops 818544640 | bytes 6063357 | solution.py:133
  462.8 8.9 conditional.8
  465.1 6.7 bitcast_add_fusion.1
  473.7 9.0 conditional.8
  475.9 6.8 bitcast_add_fusion.1
  499.5 19.6 %all-gather.15.cloned.1.call-done = bf16[768,3072]{1,0:T(8,128)(2,1)} async-done(((bf16[96,3072]{1,0:T(8,128)(2,1)}), bf16[768,3072]{1,0:T(8,128)(2,1)}) %all-gather.15.cloned.1.call-update) | async-done | bytes 4718608 | tf_op jit(solution)/shard_map/all_gather | solution.py:58
  519.1 8.1 fusion.76
  527.2 71.7 %all-gather.17.cloned.1.call-done = bf16[3072,768]{1,0:T(8,128)(2,1)} async-done(((bf16[384,768]{1,0:T(8,128)(2,1)}), bf16[3072,768]{1,0:T(8,128)(2,1)}) %all-gather.17.cloned.1.call-update) | async-done | bytes 4718608 | tf_op jit(solution)/shard_map/all_gather | solution.py:60
  598.9 9.8 fusion.83
  608.6 3.5 multiply_reduce_fusion
  618.6 125.4 %while.40 = (s32[]{:T(128)}, f32[1,512,12,64]{1,3,2,0:T(8,128)}, bf16[8,512,1,1536]{3,1,0,2:T(8,128)(2,1)}, s32[8]{0:T(128)S(1)}, s32[]{:T(128)}, /*index=5*/bf1...) while((s32[]{:T(128)}, f32[1,512,12,64]{1,3,2,0:T(8,128)}, ...), condition=%wide.region_21.22_spmd.clone, body=%wide.region_18.0_spmd.clone.sunk | while | flops 2050097152 | bytes 80298304 | solution.py:241
  620.7 35.1 %conditional.9 = (f32[1,512,12,64]{1,3,2,0:T(8,128)S(1)}, bf16[1,512,1,1536]{1,3,2,0:T(8,128)(2,1)S(1)}) conditional(s32[]{:T(128)} %convert_element_type.293, () %tuple.107, (s32[]{:T(128)}, bf16[1,4096,12,64]{1,3,2,0:T(8,128)(2,1)}, s32[1,4096]{1,0:T(1,128)S(1)}, s32[1,512]{1,0:T(1,128)S(1)}, bf16[1,512,12,64]{1,3,2,0:T(8,128)(2,1)}, ...), branch_computations={%region_19.19_spmd, %region_20.20_spmd} | conditional | flops 2049310720 | bytes 69288000 | solution.py:236
  622.9 9.6 fusion.39
  632.5 9.7 fusion.28
  642.2 7.8 fusion.32
  650.0 2.5 multiply_bitcast_fusion
  652.5 3.1 convolution_multiply_fusion
  661.1 35.1 %conditional.9 = (f32[1,512,12,64]{1,3,2,0:T(8,128)S(1)}, bf16[1,512,1,1536]{1,3,2,0:T(8,128)(2,1)S(1)}) conditional(s32[]{:T(128)} %convert_element_type.293, () %tuple.107, (s32[]{:T(128)}, bf16[1,4096,12,64]{1,3,2,0:T(8,128)(2,1)}, s32[1,4096]{1,0:T(1,128)S(1)}, s32[1,512]{1,0:T(1,128)S(1)}, bf16[1,512,12,64]{1,3,2,0:T(8,128)(2,1)}, ...), branch_computations={%region_19.19_spmd, %region_20.20_spmd} | conditional | flops 2049310720 | bytes 69288000 | solution.py:236
  663.4 9.5 fusion.39
  673.0 9.7 fusion.28
  682.7 7.8 fusion.32
  690.5 2.5 multiply_bitcast_fusion
  693.0 3.1 convolution_multiply_fusion
  696.2 2.9 select_add_fusion.2
  703.3 2.9 select_add_fusion.2
  710.4 2.9 select_add_fusion.2
  717.6 2.9 select_add_fusion.2
  724.6 2.9 select_add_fusion.2
  731.8 2.9 select_add_fusion.2
  738.9 2.9 select_add_fusion.2
  747.3 6.5 convolution_convert_fusion.3
  754.9 8.6 convolution_convert_fusion.2
  767.3 413.9 %reduce-scatter.7.cloned.1.call-done = bf16[512,1,1536]{2,0,1:T(8,128)(2,1)} async-done(((bf16[4096,1,1536]{2,0,1:T(8,128)(2,1)}), bf16[512,1,1536]{2,0,1:T(8,128)(2,1)}) %reduce-scatter.7.cloned.1.call-update) | async-done | bytes 1572880 | tf_op jit(solution)/shard_map/reduce_scatter | solution.py:243
  1181.2 5.5 convolution_convert_fusion.4
  1186.8 4.8 multiply_reduce_fusion.1
  1193.6 10.6 fusion.51
  1206.1 35.3 %all-reduce.11 = (bf16[768]{0:T(1024)(128)(2,1)S(1)}, bf16[768]{0:T(1024)(128)(2,1)S(1)}, bf16[768]{0:T(1024)(128)(2,1)S(1)}, bf16[768]{0:T(1024)(128)(2,1)S(1)}...) all-reduce(bf16[768]{0:T(1024)(128)(2,1)S(1)} %dynamic-update-slice, ...), channel_id=1, replica_groups=mesh['dp'=4,'seq'=8] {'seq'}, use_global_device_ids=true, to_apply=%add.4 | all-reduce | flops 7680 | bytes 30720
  1241.4 7.7 reduce-scatter.13.cloned.1.call-done
  1249.0 98.9 %reduce-scatter.15.cloned.1.call-done = bf16[96,3072]{1,0:T(8,128)(2,1)} async-done(((bf16[768,3072]{1,0:T(8,128)(2,1)}), bf16[96,3072]{1,0:T(8,128)(2,1)}) %reduce-scatter.15.cloned.1.call-update) | async-done | bytes 589840 | tf_op jit(solution)/shard_map/reduce_scatter | solution.py:284
  1348.0 98.9 %reduce-scatter.17.cloned.1.call-done = bf16[384,768]{1,0:T(8,128)(2,1)} async-done(((bf16[3072,768]{1,0:T(8,128)(2,1)}), bf16[384,768]{1,0:T(8,128)(2,1)}) %reduce-scatter.17.cloned.1.call-update) | async-done | bytes 589840 | tf_op jit(solution)/shard_map/reduce_scatter | solution.py:290
  1446.8 82.7 %reduce-scatter.11.cloned.1.call-done = bf16[96,2304]{1,0:T(8,128)(2,1)} async-done(((bf16[768,2304]{1,0:T(8,128)(2,1)}), bf16[96,2304]{1,0:T(8,128)(2,1)}) %reduce-scatter.11.cloned.1.call-update) | async-done | bytes 442384 | tf_op jit(solution)/shard_map/reduce_scatter | solution.py:272
  1529.6 165.2 %reduce-scatter.9.cloned.1.call-done = bf16[768,768]{0,1:T(8,128)(2,1)} async-done(((bf16[6144,768]{0,1:T(8,128)(2,1)}), bf16[768,768]{0,1:T(8,128)(2,1)}) %reduce-scatter.9.cloned.1.call-update) | async-done | bytes 1179664 | tf_op jit(solution)/shard_map/reduce_scatter | solution.py:263
  1694.8 9.0 fusion.64
  1704.3 7.3 all-reduce.13
  1714.7 10.8 fusion.52
  1725.4 36.6 %all-reduce.17.cloned.1.call-done = (bf16[768,768]{0,1:T(8,128)(2,1)}, bf16[96,2304]{1,0:T(8,128)(2,1)}, bf16[96,768]{1,0:T(8,128)(2,1)}, bf16[96,3072]{1,0:T(8,128)(2,1)}, bf16[384,768]{1,0:T(8,128)(2,1)}) async-done(((bf16[768,768]{0,1:T(8,128)(2,1)}, bf16[96,2304]{1,0:T(8,128)(2,1)}, bf16[96,768]{1,0:T(8,128)(2,1)}, bf16[96,3072]{1,0:T(8,128)(2,1)}, bf16[384,768]{1,0:T(8,128)(2,1)}), ...) | async-done | bytes 2949136 | tf_op jit(solution)/shard_map/psum | solution.py:298
  1765.8 2.7 copy.73
  (277 shorter events, 82.7 us)
Async XLA Ops:
  7.2 143.5 %all-gather.9.cloned.1.call-start = ((), (), s32[]{:S(2)}) async-start(), calls=%async_computation.6 | async-start | bytes 10616832 | tf_op jit(solution)/shard_map/all_gather | solution.py:51
  7.9 207.8 %all-gather.11.cloned.1.call-start = ((), (), s32[]{:S(2)}) async-start(), calls=%async_computation.7 | async-start | bytes 3981312 | tf_op jit(solution)/shard_map/all_gather | solution.py:54
  8.7 388.9 %all-gather.19.cloned.1.call-start = ((), (), s32[]{:S(2)}) async-start(), calls=%async_computation.17 | async-start | bytes 14155776 | tf_op jit(solution)/shard_map/all_gather | solution.py:84
  38.7 177.0 %copy-start.34 = (f32[768]{0:T(1024)}, f32[768]{0:T(1024)S(1)}, u32[]{:S(2)}) copy-start(f32[768]{0:T(1024)S(1)} %convert_element_type.201) | copy-start | bytes 9220
  38.7 177.0 %copy-start.27 = (f32[768]{0:T(1024)}, f32[768]{0:T(1024)S(1)}, u32[]{:S(2)}) copy-start(f32[768]{0:T(1024)S(1)} %convert_element_type.200) | copy-start | bytes 9220
  160.4 335.2 %copy-start.1 = (f32[512,768]{1,0:T(8,128)}, f32[512,768]{1,0:T(8,128)S(1)}, u32[]{:S(2)}) copy-start(f32[512,768]{1,0:T(8,128)S(1)} %get-tuple-element.512) | copy-start | bytes 4718596
  160.5 59.4 %copy-start.21 = (f32[512]{0:T(512)}, f32[512]{0:T(512)S(1)}, u32[]{:S(2)}) copy-start(f32[512]{0:T(512)S(1)} %broadcast_multiply_fusion.1) | copy-start | bytes 6148
  160.8 59.1 %copy-start.23 = (f32[512]{0:T(512)}, f32[512]{0:T(512)S(1)}, u32[]{:S(2)}) copy-start(f32[512]{0:T(512)S(1)} %multiply_reduce_fusion.6) | copy-start | bytes 6148
  160.8 59.1 %copy-start.31 = (f32[512]{0:T(512)}, f32[512]{0:T(512)S(1)}, u32[]{:S(2)}) copy-start(f32[512]{0:T(512)S(1)} %fusion.72) | copy-start | bytes 6148
  219.8 1.4 copy-start.14
  221.3 3.1 copy-start.40
  221.3 30.3 %copy-start.20 = (s32[1,4096]{1,0:T(1,128)S(1)}, s32[1,4096]{1,0:T(1,128)}, u32[]{:S(2)}) copy-start(s32[1,4096]{1,0:T(1,128)} %param.38) | copy-start | bytes 49156
  222.5 30.9 %slice-start = ((bf16[512,2304]{1,0:T(8,128)(2,1)}), bf16[512,768]{1,0:T(8,128)(2,1)S(1)}, s32[]{:S(2)}) async-start(bf16[512,2304]{1,0:T(8,128)(2,1)} %copy-done.14), calls=%async_computation.19 | async-start | bytes 1572864 | tf_op jit(solution)/shard_map/slice | solution.py:82
  222.5 273.1 %all-gather.13.cloned.1.call-start = ((), (), s32[]{:S(2)}) async-start(), calls=%async_computation.8 | async-start | bytes 1327104 | tf_op jit(solution)/shard_map/all_gather | solution.py:55
  223.1 296.0 %all-gather.15.cloned.1.call-start = ((), (), s32[]{:S(2)}) async-start(), calls=%async_computation.9 | async-start | bytes 5308416 | tf_op jit(solution)/shard_map/all_gather | solution.py:58
  223.7 375.2 %all-gather.17.cloned.1.call-start = ((), (), s32[]{:S(2)}) async-start(), calls=%async_computation.10 | async-start | bytes 5308416 | tf_op jit(solution)/shard_map/all_gather | solution.py:60
  224.3 956.9 %reduce-scatter.7.cloned.1.call-start = ((), (), s32[]{:S(2)}) async-start(), calls=%async_computation.11 | async-start | bytes 14155776 | tf_op jit(solution)/shard_map/reduce_scatter | solution.py:243
  224.4 294.7 %copy-start.36 = (f32[768]{0:T(1024)}, f32[768]{0:T(1024)S(1)}, u32[]{:S(2)}) copy-start(f32[768]{0:T(1024)S(1)} %convert_element_type.207) | copy-start | bytes 9220
  251.5 347.4 %copy-start.29 = (f32[8,1,384]{2,1,0:T(1,128)}, f32[8,1,384]{2,1,0:T(1,128)S(1)}, u32[]{:S(2)}) copy-start(f32[8,1,384]{2,1,0:T(1,128)S(1)} %convert_element_type.243) | copy-start | bytes 36868
  498.1 1.1 copy-start.3
  499.5 99.4 %copy-start.9 = (bf16[1,512,768]{2,1,0:T(8,128)(2,1)S(1)}, bf16[1,512,768]{2,1,0:T(8,128)(2,1)}, u32[]{:S(2)}) copy-start(bf16[1,512,768]{2,1,0:T(8,128)(2,1)} %param.39) | copy-start | bytes 2359300
  598.9 9.8 copy-start.4
  598.9 9.8 copy-start.41
  608.6 3.5 copy-start.43
  612.2 3.0 copy-start.15
  612.8 1.2 copy-start.7
  612.9 3.1 copy-start.25
  614.3 0.9 copy-start.16
  744.0 1.1 copy-start.13
  744.0 1.4 copy-start.17
  744.1 3.2 copy-start.5
  744.1 3.2 copy-start.37
  744.1 504.9 %reduce-scatter.13.cloned.1.call-start = ((), (), s32[]{:S(2)}) async-start(), calls=%async_computation.14 | async-start | bytes 1327104 | tf_op jit(solution)/shard_map/reduce_scatter | solution.py:275
  747.2 600.7 %reduce-scatter.15.cloned.1.call-start = ((), (), s32[]{:S(2)}) async-start(), calls=%async_computation.15 | async-start | bytes 5308416 | tf_op jit(solution)/shard_map/reduce_scatter | solution.py:284
  753.8 1.1 copy-start.10
  753.8 1.1 copy-start.30
  753.8 693.1 %reduce-scatter.17.cloned.1.call-start = ((), (), s32[]{:S(2)}) async-start(), calls=%async_computation.16 | async-start | bytes 5308416 | tf_op jit(solution)/shard_map/reduce_scatter | solution.py:290
  763.5 1.4 copy-start
  763.5 417.7 %copy-start.2 = (f32[512,768]{1,0:T(8,128)S(1)}, f32[512,768]{1,0:T(8,128)}, u32[]{:S(2)}) copy-start(f32[512,768]{1,0:T(8,128)} %copy-done.1) | copy-start | bytes 4718596
  763.5 417.7 %copy-start.22 = (f32[512]{0:T(512)S(1)}, f32[512]{0:T(512)}, u32[]{:S(2)}) copy-start(f32[512]{0:T(512)} %copy-done.21) | copy-start | bytes 6148
  763.5 417.7 %copy-start.28 = (f32[768]{0:T(1024)S(1)}, f32[768]{0:T(1024)}, u32[]{:S(2)}) copy-start(f32[768]{0:T(1024)} %copy-done.27) | copy-start | bytes 9220
  763.5 417.7 %copy-start.32 = (f32[512]{0:T(512)S(1)}, f32[512]{0:T(512)}, u32[]{:S(2)}) copy-start(f32[512]{0:T(512)} %copy-done.31) | copy-start | bytes 6148
  763.5 417.7 %copy-start.35 = (f32[768]{0:T(1024)S(1)}, f32[768]{0:T(1024)}, u32[]{:S(2)}) copy-start(f32[768]{0:T(1024)} %copy-done.34) | copy-start | bytes 9220
  763.5 766.0 %reduce-scatter.11.cloned.1.call-start = ((), (), s32[]{:S(2)}) async-start(), calls=%async_computation.13 | async-start | bytes 3981312 | tf_op jit(solution)/shard_map/reduce_scatter | solution.py:272
  1186.7 4.9 copy-start.24
  1186.7 508.0 %reduce-scatter.9.cloned.1.call-start = ((), (), s32[]{:S(2)}) async-start(), calls=%async_computation.12 | async-start | bytes 10616832 | tf_op jit(solution)/shard_map/reduce_scatter | solution.py:263
  1191.6 1.4 copy-start.8
  1191.6 1.6 copy-start.11
  1191.6 1.6 copy-start.26
  1204.1 1.6 copy-start.12
  1204.1 1.7 copy-start.42
  1204.1 2.0 copy-start.33
  1204.2 2.0 copy-start.38
  1204.2 2.0 copy-start.39
  1204.2 490.6 %copy-start.6 = (f32[512,768]{1,0:T(8,128)S(1)}, f32[512,768]{1,0:T(8,128)}, u32[]{:S(2)}) copy-start(f32[512,768]{1,0:T(8,128)} %copy-done.3) | copy-start | bytes 4718596
  1204.2 557.9 %all-reduce.17.cloned.1.call-start = ((), (), s32[]{:S(2)}) async-start(), calls=%async_computation.18 | async-start | bytes 5898240 | tf_op jit(solution)/shard_map/psum | solution.py:298
  1762.1 6.5 copy-start.19
  1763.8 5.9 copy-start.18
Sparse Core Ops, SparseCore 0:
  10.2 140.4 all-gather.8
  152.9 62.7 all-gather.10
  222.7 174.8 all-gather.18
  399.6 39.2 all-gather.12
  441.0 78.0 all-gather.14
  521.1 77.6 all-gather.16
  744.2 436.9 reduce-scatter.6
  1185.1 63.8 reduce-scatter.12
  1253.3 94.6 reduce-scatter.14
  1351.5 95.3 reduce-scatter.16
  1450.5 79.0 reduce-scatter.10
  1533.0 161.7 reduce-scatter.8
  1697.5 64.5 all-reduce.16
where the time goes:
time: 1790 us; the launch traced here: 1780 us
  waiting for transfers between devices  1310 us (73%)
  matrix products  185 us (10%)
  blocking collectives  94.2 us (5%)
  local copies, waits for them, and re-layouts  82.7 us (5%)
  other arithmetic  45.2 us (3%)
  loops' own time  44.7 us (2%)
    reduce_scatter x1, waiting for transfers between devices, per_device(): lax.psum_scatter(every_pair.astype(jnp.bfloat16), 'seq', scatter_dimensio...  414 us
    reduce_scatter x1, waiting for transfers between devices, per_device(): lax.psum_scatter(embedding_grad.astype(jnp.bfloat16), 'seq', scatter_dime...  165 us
    all_gather x1, waiting for transfers between devices, per_device(): sequence_pairs = lax.all_gather(local_pairs, 'seq', axis=1, tiled=True)  143 us
    all_gather x1, waiting for transfers between devices, per_device(): lax.all_gather(embedding, 'seq', axis=0, tiled=True)  112 us
    reduce_scatter x1, waiting for transfers between devices, per_device(): lax.psum_scatter(up_weight_grad.astype(jnp.bfloat16), 'seq', scatter_dime...  98.9 us
    reduce_scatter x1, waiting for transfers between devices, per_device(): lax.psum_scatter(down_weight_grad.astype(jnp.bfloat16), 'seq', scatter_di...  98.9 us
    reduce_scatter x1, waiting for transfers between devices, per_device(): lax.psum_scatter(joint_weight_grad.astype(jnp.bfloat16), 'seq', scatter_d...  82.7 us
    all_gather x1, waiting for transfers between devices, per_device(): lax.all_gather(down_weight, 'seq', axis=0, tiled=True)  71.7 us
  transfers between devices with their start and end apart: 13, of which 12 were waited for; matrix products, arithmetic and copies ran while one was open for 9% of the time, Pallas kernels for 0%

commit v1 on v0

--- a/solution.py
+++ b/solution.py
@@ -3,6 +3,7 @@
 import jax.numpy as jnp
 from jax import lax
 from jax.sharding import PartitionSpec as P
+from jax.lax import axis_index, axis_size, ppermute
 
 HEADS = 12
 HEAD_DIM = 64
@@ -47,11 +48,33 @@
     count_rows = seqs_here * rows_here
     length = block_number.shape[1]
     scale = HEAD_DIM ** (-0.5)
+
+    def form_the_ticks(in_array, lane_axis, out_dim):
+        clean = axis_size(lane_axis)
+        y_new = axis_index(lane_axis)
+        response, raw_out, part_next = (clean, y_new, in_array.shape[out_dim])
+        prior, known = (in_array, 1)
+        while known < response:
+            prior = jnp.concatenate(
+                [
+                    prior,
+                    ppermute(
+                        prior,
+                        axis_name=lane_axis,
+                        perm=[(hop_no, (hop_no - known) % response) for hop_no in range(response)],
+                    ),
+                ],
+                out_dim,
+            )
+            known = 2 * known
+        piece_now = jnp.roll(prior, raw_out * part_next, axis=out_dim)
+        return piece_now
+
     gathered_params = (
         lax.all_gather(embedding, "seq", axis=0, tiled=True),
         lax.all_gather(first_gain, "seq", axis=0, tiled=True),
         lax.all_gather(first_shift, "seq", axis=0, tiled=True),
-        lax.all_gather(joint_weight, "seq", axis=0, tiled=True),
+        form_the_ticks(joint_weight, "seq", 0),
         lax.all_gather(output_weight, "seq", axis=0, tiled=True),
         lax.all_gather(second_gain, "seq", axis=0, tiled=True),
         lax.all_gather(second_shift, "seq", axis=0, tiled=True),

time: 1790 us -> 1910 us (1.067)
  blocking collectives: 94.2 us -> 171 us
  waiting for transfers between devices: 1310 us -> 1330 us
    ppermute x0 -> x3, waiting for transfers between devices: none -> 123 us  [form_the_ticks(): ppermute(prior, axis_name=lane_axis, perm=[(hop_no, (hop_no - known) % re...]
    all_gather x1, waiting for transfers between devices: 112 us -> 0.01 us  [per_device(): lax.all_gather(embedding, 'seq', axis=0, tiled=True)]
    unnamed x2, blocking collectives: 59.8 us -> 124 us
  transfers between devices with their start and end apart: 13 -> 16, of which waited for: 12 -> 14; matrix products, arithmetic and copies ran while one was open for 9% -> 9% of each run, Pallas kernels for 0% -> 0%
where the time goes in v1:
time: 1910 us; the launch traced here: 1900 us
  waiting for transfers between devices  1330 us (70%)
  matrix products  185 us (10%)
  blocking collectives  171 us (9%)
  local copies, waits for them, and re-layouts  88.1 us (5%)
  other arithmetic  49.9 us (3%)
  loops' own time  44.7 us (2%)
    reduce_scatter x1, waiting for transfers between devices, per_device(): lax.psum_scatter(every_pair.astype(jnp.bfloat16), 'seq', scatter_dimensio...  414 us
    reduce_scatter x1, waiting for transfers between devices, per_device(): lax.psum_scatter(embedding_grad.astype(jnp.bfloat16), 'seq', scatter_dime...  165 us
    all_gather x1, waiting for transfers between devices, per_device(): sequence_pairs = lax.all_gather(local_pairs, 'seq', axis=1, tiled=True)  146 us
    unnamed x2, blocking collectives  124 us
    ppermute x3, waiting for transfers between devices, form_the_ticks(): ppermute(prior, axis_name=lane_axis, perm=[(hop_no, (hop_no - known) % re...  123 us
    reduce_scatter x1, waiting for transfers between devices, per_device(): lax.psum_scatter(up_weight_grad.astype(jnp.bfloat16), 'seq', scatter_dime...  98.9 us
    reduce_scatter x1, waiting for transfers between devices, per_device(): lax.psum_scatter(down_weight_grad.astype(jnp.bfloat16), 'seq', scatter_di...  98.8 us
    reduce_scatter x1, waiting for transfers between devices, per_device(): lax.psum_scatter(joint_weight_grad.astype(jnp.bfloat16), 'seq', scatter_d...  82.7 us
  transfers between devices with their start and end apart: 16, of which 14 were waited for; matrix products, arithmetic and copies ran while one was open for 9% of the time, Pallas kernels for 0%

profile of v1, /device:TPU:0, one launch (start us, length us, event | category | flops | bytes accessed | tf_op | source)
XLA Modules:
  0.0 1896.5 jit_solution(11239641198370974155)
XLA Ops:
  8.0 6.1 collective-permute-start
  14.1 12.2 collective-permute-done
  27.5 53.9 %collective-permute-done.1 = bf16[192,2304]{1,0:T(8,128)(2,1)S(1)} collective-permute-done((bf16[192,2304]{1,0:T(8,128)(2,1)S(1)}, bf16[192,2304]{1,0:T(8,128)(2,1)S(1)}, u32[]{:S(2)}, u32[]{:S(2)}) %collective-permute-start.1) | collective-permute-done | bytes 884768 | tf_op jit(solution)/shard_map/ppermute | solution.py:61
  86.5 88.8 %all-reduce.12 = (bf16[768]{0:T(1024)(128)(2,1)}, bf16[768]{0:T(1024)(128)(2,1)}, bf16[768]{0:T(1024)(128)(2,1)}, bf16[768]{0:T(1024)(128)(2,1)}) all-reduce(bf16[768]{0:T(1024)(128)(2,1)S(1)} %dynamic-update-slice.1, bf16[768]{0:T(1024)(128)(2,1)S(1)} %dynamic-update-slice, ...), channel_id=1, replica_groups=mesh['dp'=4,'seq'=8] {'seq'}, use_global_device_ids=true, to_apply=%add.1 | all-reduce | flops 3072 | bytes 12288
  179.3 57.2 %collective-permute-done.2 = bf16[384,2304]{1,0:T(8,128)(2,1)S(1)} collective-permute-done((bf16[384,2304]{1,0:T(8,128)(2,1)}, bf16[384,2304]{1,0:T(8,128)(2,1)S(1)}, u32[]{:S(2)}, u32[]{:S(2)}) %collective-permute-start.2) | collective-permute-done | bytes 1769504 | tf_op jit(solution)/shard_map/ppermute | solution.py:61
  241.8 9.7 fusion.83
  252.6 4.2 convolution_convert_fusion.5
  261.6 40.5 %all-gather.1 = bf16[8,1,384]{2,1,0:T(2,128)(2,1)S(1)} all-gather(bf16[1,1,384]{2,1,0:T(2,128)(2,1)S(1)} %reshape.385), channel_id=1, replica_groups=mesh['dp'=4,'seq'=8] {'seq'}, dimensions={0}, use_global_device_ids=true | all-gather | bytes 6912 | tf_op jit(solution)/shard_map/all_gather | solution.py:82
  305.1 145.7 %all-gather.19.cloned.1.call-done = bf16[4096,1536]{1,0:T(8,128)(2,1)} async-done(((bf16[512,1536]{1,0:T(8,128)(2,1)}), bf16[4096,1536]{1,0:T(8,128)(2,1)}) %all-gather.19.cloned.1.call-update) | async-done | bytes 12582928 | tf_op jit(solution)/shard_map/all_gather | solution.py:107
  450.8 10.3 fusion.81
  461.1 8.8 copy.68
  469.9 8.6 copy.67
  478.5 35.6 %while.38 = (s32[]{:T(128)}, f32[1,12,512]{2,1,0:T(8,128)S(1)}, f32[1,12,512]{2,1,0:T(8,128)S(1)}, s32[8]{0:T(128)S(1)}, s32[]{:T(128)}, /*index=5*/s32[1,4096]{...) while((s32[]{:T(128)}, f32[1,12,512]{2,1,0:T(8,128)S(1)}, ...), condition=%wide.region_8.9_spmd, body=%wide.region_3.8_spmd.sunk | while | flops 424947712 | bytes 27853072 | solution.py:139
  480.4 10.1 conditional.7
  482.7 5.2 fusion
  488.0 2.6 exponential_reduce_fusion
  492.5 10.1 conditional.7
  494.7 5.2 fusion
  514.4 33.7 %while.39 = (s32[]{:T(128)}, f32[1,512,12,64]{1,3,2,0:T(8,128)S(1)}, s32[8]{0:T(128)S(1)}, s32[]{:T(128)}, bf16[1,4096,12,64]{1,3,2,0:T(8,128)(2,1)}, /*index=5*...) while((s32[]{:T(128)}, ...), condition=%wide.region_12.13_spmd, body=%wide.region_9.12_spmd.sunk | while | flops 818544640 | bytes 6063357 | solution.py:156
  516.3 8.9 conditional.8
  518.5 6.7 bitcast_add_fusion.1
  527.1 9.0 conditional.8
  529.4 6.7 bitcast_add_fusion.1
  552.9 19.5 %all-gather.13.cloned.1.call-done = bf16[768,3072]{1,0:T(8,128)(2,1)} async-done(((bf16[96,3072]{1,0:T(8,128)(2,1)}), bf16[768,3072]{1,0:T(8,128)(2,1)}) %all-gather.13.cloned.1.call-update) | async-done | bytes 4718608 | tf_op jit(solution)/shard_map/all_gather | solution.py:81
  572.4 8.1 fusion.78
  580.5 71.7 %all-gather.15.cloned.1.call-done = bf16[3072,768]{1,0:T(8,128)(2,1)} async-done(((bf16[384,768]{1,0:T(8,128)(2,1)}), bf16[3072,768]{1,0:T(8,128)(2,1)}) %all-gather.15.cloned.1.call-update) | async-done | bytes 4718608 | tf_op jit(solution)/shard_map/all_gather | solution.py:83
  652.2 9.8 fusion.85
  662.0 3.5 multiply_reduce_fusion
  671.9 125.4 %while.40 = (s32[]{:T(128)}, f32[1,512,12,64]{1,3,2,0:T(8,128)}, bf16[8,512,1,1536]{3,1,0,2:T(8,128)(2,1)}, s32[8]{0:T(128)S(1)}, s32[]{:T(128)}, /*index=5*/bf1...) while((s32[]{:T(128)}, f32[1,512,12,64]{1,3,2,0:T(8,128)}, ...), condition=%wide.region_21.22_spmd.clone, body=%wide.region_18.21_spmd.clone.sunk | while | flops 2050097152 | bytes 80298304 | solution.py:264
  673.9 35.1 %conditional.9 = (f32[1,512,12,64]{1,3,2,0:T(8,128)S(1)}, bf16[1,512,1,1536]{1,3,2,0:T(8,128)(2,1)S(1)}) conditional(s32[]{:T(128)} %convert_element_type.293, () %tuple.107, (s32[]{:T(128)}, bf16[1,4096,12,64]{1,3,2,0:T(8,128)(2,1)}, s32[1,4096]{1,0:T(1,128)S(1)}, s32[1,512]{1,0:T(1,128)S(1)}, bf16[1,512,12,64]{1,3,2,0:T(8,128)(2,1)}, ...), branch_computations={%region_19.19_spmd, %region_20.20_spmd} | conditional | flops 2049310720 | bytes 69288000 | solution.py:259
  676.2 9.5 fusion.39
  685.7 9.7 fusion.28
  695.5 7.8 fusion.32
  705.8 3.1 convolution_multiply_fusion
  714.4 35.1 %conditional.9 = (f32[1,512,12,64]{1,3,2,0:T(8,128)S(1)}, bf16[1,512,1,1536]{1,3,2,0:T(8,128)(2,1)S(1)}) conditional(s32[]{:T(128)} %convert_element_type.293, () %tuple.107, (s32[]{:T(128)}, bf16[1,4096,12,64]{1,3,2,0:T(8,128)(2,1)}, s32[1,4096]{1,0:T(1,128)S(1)}, s32[1,512]{1,0:T(1,128)S(1)}, bf16[1,512,12,64]{1,3,2,0:T(8,128)(2,1)}, ...), branch_computations={%region_19.19_spmd, %region_20.20_spmd} | conditional | flops 2049310720 | bytes 69288000 | solution.py:259
  716.7 9.6 fusion.39
  726.2 9.7 fusion.28
  735.9 7.8 fusion.32
  746.2 3.1 convolution_multiply_fusion
  749.5 2.9 select_add_fusion.2
  756.6 2.9 select_add_fusion.2
  763.6 2.9 select_add_fusion.2
  770.8 2.9 select_add_fusion.2
  777.9 2.9 select_add_fusion.2
  785.0 2.9 select_add_fusion.2
  792.1 2.9 select_add_fusion.2
  800.5 6.5 convolution_convert_fusion.3
  808.1 8.6 convolution_convert_fusion.2
  820.4 414.2 %reduce-scatter.7.cloned.1.call-done = bf16[512,1,1536]{2,0,1:T(8,128)(2,1)} async-done(((bf16[4096,1,1536]{2,0,1:T(8,128)(2,1)}), bf16[512,1,1536]{2,0,1:T(8,128)(2,1)}) %reduce-scatter.7.cloned.1.call-update) | async-done | bytes 1572880 | tf_op jit(solution)/shard_map/reduce_scatter | solution.py:266
  1234.6 5.4 convolution_convert_fusion.4
  1240.1 60.4 %all-gather.17.cloned.1.call-done = bf16[768,2304]{1,0:T(8,128)(2,1)} async-done(((bf16[96,2304]{1,0:T(8,128)(2,1)}), bf16[768,2304]{1,0:T(8,128)(2,1)}) %all-gather.17.cloned.1.call-update) | async-done | bytes 3538960 | tf_op jit(solution)/shard_map/all_gather | solution.py:174
  1300.5 4.8 multiply_reduce_fusion.1
  1307.3 10.6 fusion.51
  1319.8 34.9 %all-reduce.11 = (bf16[768]{0:T(1024)(128)(2,1)S(1)}, bf16[768]{0:T(1024)(128)(2,1)S(1)}, bf16[768]{0:T(1024)(128)(2,1)S(1)}, bf16[768]{0:T(1024)(128)(2,1)S(1)}...) all-reduce(bf16[768]{0:T(1024)(128)(2,1)S(1)} %dynamic-update-slice, ...), channel_id=1, replica_groups=mesh['dp'=4,'seq'=8] {'seq'}, use_global_device_ids=true, to_apply=%add.4 | all-reduce | flops 7680 | bytes 30720
  1354.7 13.3 reduce-scatter.13.cloned.1.call-done
  1368.0 98.9 %reduce-scatter.15.cloned.1.call-done = bf16[96,3072]{1,0:T(8,128)(2,1)} async-done(((bf16[768,3072]{1,0:T(8,128)(2,1)}), bf16[96,3072]{1,0:T(8,128)(2,1)}) %reduce-scatter.15.cloned.1.call-update) | async-done | bytes 589840 | tf_op jit(solution)/shard_map/reduce_scatter | solution.py:307
  1466.9 98.8 %reduce-scatter.17.cloned.1.call-done = bf16[384,768]{1,0:T(8,128)(2,1)} async-done(((bf16[3072,768]{1,0:T(8,128)(2,1)}), bf16[384,768]{1,0:T(8,128)(2,1)}) %reduce-scatter.17.cloned.1.call-update) | async-done | bytes 589840 | tf_op jit(solution)/shard_map/reduce_scatter | solution.py:313
  1565.7 82.7 %reduce-scatter.11.cloned.1.call-done = bf16[96,2304]{1,0:T(8,128)(2,1)} async-done(((bf16[768,2304]{1,0:T(8,128)(2,1)}), bf16[96,2304]{1,0:T(8,128)(2,1)}) %reduce-scatter.11.cloned.1.call-update) | async-done | bytes 442384 | tf_op jit(solution)/shard_map/reduce_scatter | solution.py:295
  1648.4 165.2 %reduce-scatter.9.cloned.1.call-done = bf16[768,768]{0,1:T(8,128)(2,1)} async-done(((bf16[6144,768]{0,1:T(8,128)(2,1)}), bf16[768,768]{0,1:T(8,128)(2,1)}) %reduce-scatter.9.cloned.1.call-update) | async-done | bytes 1179664 | tf_op jit(solution)/shard_map/reduce_scatter | solution.py:286
  1813.6 9.0 fusion.65
  1823.1 7.3 all-reduce.13
  1833.5 10.8 fusion.52
  1844.3 36.6 %all-reduce.17.cloned.1.call-done = (bf16[768,768]{0,1:T(8,128)(2,1)}, bf16[96,2304]{1,0:T(8,128)(2,1)}, bf16[96,768]{1,0:T(8,128)(2,1)}, bf16[96,3072]{1,0:T(8,128)(2,1)}, bf16[384,768]{1,0:T(8,128)(2,1)}) async-done(((bf16[768,768]{0,1:T(8,128)(2,1)}, bf16[96,2304]{1,0:T(8,128)(2,1)}, bf16[96,768]{1,0:T(8,128)(2,1)}, bf16[96,3072]{1,0:T(8,128)(2,1)}, bf16[384,768]{1,0:T(8,128)(2,1)}), ...) | async-done | bytes 2949136 | tf_op jit(solution)/shard_map/psum | solution.py:321
  1884.6 2.7 copy.73
  (307 shorter events, 100.4 us)
Async XLA Ops:
  7.2 76.5 %copy-start.43 = (u32[32]{0:T(128)S(1)}, u32[32]{0:T(128)}, u32[]{:S(2)}) copy-start(u32[32]{0:T(128)} %constant.120) | copy-start | bytes 388
  7.2 169.5 %copy-start.9 = (bf16[96,2304]{1,0:T(8,128)(2,1)S(1)}, bf16[96,2304]{1,0:T(8,128)(2,1)}, u32[]{:S(2)}) copy-start(bf16[96,2304]{1,0:T(8,128)(2,1)} %param.30) | copy-start | bytes 1327108
  7.2 77.7 %copy-start.46 = (bf16[96]{0:T(256)(128)(2,1)S(1)}, bf16[96]{0:T(256)(128)(2,1)}, u32[]{:S(2)}) copy-start(bf16[96]{0:T(256)(128)(2,1)} %param.32) | copy-start | bytes 580
  7.2 78.0 %copy-start.47 = (bf16[96]{0:T(256)(128)(2,1)S(1)}, bf16[96]{0:T(256)(128)(2,1)}, u32[]{:S(2)}) copy-start(bf16[96]{0:T(256)(128)(2,1)} %param.33) | copy-start | bytes 580
  7.2 78.2 %copy-start.48 = (bf16[96]{0:T(256)(128)(2,1)S(1)}, bf16[96]{0:T(256)(128)(2,1)}, u32[]{:S(2)}) copy-start(bf16[96]{0:T(256)(128)(2,1)} %param.28) | copy-start | bytes 580
  7.2 234.5 %all-gather.9.cloned.1.call-start = ((), (), s32[]{:S(2)}) async-start(), calls=%async_computation.6 | async-start | bytes 10616832 | tf_op jit(solution)/shard_map/all_gather | solution.py:74
  8.0 442.8 %all-gather.19.cloned.1.call-start = ((), (), s32[]{:S(2)}) async-start(), calls=%async_computation.17 | async-start | bytes 14155776 | tf_op jit(solution)/shard_map/all_gather | solution.py:107
  8.0 18.3 collective-permute-start
  27.4 53.9 %collective-permute-start.1 = (bf16[192,2304]{1,0:T(8,128)(2,1)S(1)}, bf16[192,2304]{1,0:T(8,128)(2,1)S(1)}, u32[]{:S(2)}, u32[]{:S(2)}) collective-permute-start(bf16[192,2304]{1,0:T(8,128)(2,1)S(1)} %pad_maximum_fusion.4), channel_id=1, source_target_pairs={{0,6},{1,7},{2,0},{3,1},{4,2},{5,3},{6,4},{7,5},{8,14},{9,15},{10,... | collective-permute-start | bytes 2654216 | tf_op jit(solution)/shard_map/ppermute | solution.py:61
  83.7 152.8 %collective-permute-start.2 = (bf16[384,2304]{1,0:T(8,128)(2,1)}, bf16[384,2304]{1,0:T(8,128)(2,1)S(1)}, u32[]{:S(2)}, u32[]{:S(2)}) collective-permute-start(bf16[384,2304]{1,0:T(8,128)(2,1)} %pad_maximum_fusion.1), channel_id=1, source_target_pairs={{0,4},{1,5},{2,6},{3,7},{4,0},{5,1},{6,2},{7,3},{8,12},{9,13},{10,... | collective-permute-start | bytes 5308424 | tf_op jit(solution)/shard_map/ppermute | solution.py:61
  176.0 76.6 %copy-start.35 = (f32[768]{0:T(1024)}, f32[768]{0:T(1024)S(1)}, u32[]{:S(2)}) copy-start(f32[768]{0:T(1024)S(1)} %convert_element_type.201) | copy-start | bytes 9220
  176.7 75.9 %copy-start.28 = (f32[768]{0:T(1024)}, f32[768]{0:T(1024)S(1)}, u32[]{:S(2)}) copy-start(f32[768]{0:T(1024)S(1)} %convert_element_type.200) | copy-start | bytes 9220
  251.5 297.5 %copy-start.1 = (f32[512,768]{1,0:T(8,128)}, f32[512,768]{1,0:T(8,128)S(1)}, u32[]{:S(2)}) copy-start(f32[512,768]{1,0:T(8,128)S(1)} %get-tuple-element.512) | copy-start | bytes 4718596
  251.5 5.3 copy-start.22
  252.6 4.2 copy-start.32
  256.8 1.4 copy-start.15
  258.2 3.3 copy-start.44
  258.2 3.3 copy-start.42
  258.2 3.3 copy-start.41
  258.2 43.8 %copy-start.21 = (s32[1,4096]{1,0:T(1,128)S(1)}, s32[1,4096]{1,0:T(1,128)}, u32[]{:S(2)}) copy-start(s32[1,4096]{1,0:T(1,128)} %param.38) | copy-start | bytes 49156
  259.5 44.5 %slice-start = ((bf16[512,2304]{1,0:T(8,128)(2,1)}), bf16[512,768]{1,0:T(8,128)(2,1)S(1)}, s32[]{:S(2)}) async-start(bf16[512,2304]{1,0:T(8,128)(2,1)} %copy-done.15), calls=%async_computation.19 | async-start | bytes 1572864 | tf_op jit(solution)/shard_map/slice | solution.py:105
  259.5 289.5 %all-gather.11.cloned.1.call-start = ((), (), s32[]{:S(2)}) async-start(), calls=%async_computation.7 | async-start | bytes 1327104 | tf_op jit(solution)/shard_map/all_gather | solution.py:78
  260.3 312.1 %all-gather.13.cloned.1.call-start = ((), (), s32[]{:S(2)}) async-start(), calls=%async_computation.8 | async-start | bytes 5308416 | tf_op jit(solution)/shard_map/all_gather | solution.py:81
  260.8 391.3 %all-gather.15.cloned.1.call-start = ((), (), s32[]{:S(2)}) async-start(), calls=%async_computation.9 | async-start | bytes 5308416 | tf_op jit(solution)/shard_map/all_gather | solution.py:83
  261.4 973.2 %reduce-scatter.7.cloned.1.call-start = ((), (), s32[]{:S(2)}) async-start(), calls=%async_computation.10 | async-start | bytes 14155776 | tf_op jit(solution)/shard_map/reduce_scatter | solution.py:266
  261.6 310.8 %copy-start.37 = (f32[768]{0:T(1024)}, f32[768]{0:T(1024)S(1)}, u32[]{:S(2)}) copy-start(f32[768]{0:T(1024)S(1)} %convert_element_type.207) | copy-start | bytes 9220
  302.0 350.1 %copy-start.30 = (f32[8,1,384]{2,1,0:T(1,128)}, f32[8,1,384]{2,1,0:T(1,128)S(1)}, u32[]{:S(2)}) copy-start(f32[8,1,384]{2,1,0:T(1,128)S(1)} %convert_element_type.243) | copy-start | bytes 36868
  551.5 1.1 copy-start.3
  552.9 99.3 %copy-start.10 = (bf16[1,512,768]{2,1,0:T(8,128)(2,1)S(1)}, bf16[1,512,768]{2,1,0:T(8,128)(2,1)}, u32[]{:S(2)}) copy-start(bf16[1,512,768]{2,1,0:T(8,128)(2,1)} %param.39) | copy-start | bytes 2359300
  652.2 9.8 copy-start.4
  652.2 9.8 copy-start.45
  662.0 3.5 copy-start.50
  665.5 3.0 copy-start.16
  666.2 1.1 copy-start.7
  666.2 4.3 copy-start.26
  797.2 1.1 copy-start.14
  797.2 1.4 copy-start.18
  797.3 3.2 copy-start.5
  797.3 3.2 copy-start.38
  797.3 503.2 %all-gather.17.cloned.1.call-start = ((), (), s32[]{:S(2)}) async-start(), calls=%async_computation.11 | async-start | bytes 3981312 | tf_op jit(solution)/shard_map/all_gather | solution.py:174
  798.0 570.0 %reduce-scatter.13.cloned.1.call-start = ((), (), s32[]{:S(2)}) async-start(), calls=%async_computation.14 | async-start | bytes 1327104 | tf_op jit(solution)/shard_map/reduce_scatter | solution.py:298
  800.4 666.5 %reduce-scatter.15.cloned.1.call-start = ((), (), s32[]{:S(2)}) async-start(), calls=%async_computation.15 | async-start | bytes 5308416 | tf_op jit(solution)/shard_map/reduce_scatter | solution.py:307
  807.0 758.7 %reduce-scatter.17.cloned.1.call-start = ((), (), s32[]{:S(2)}) async-start(), calls=%async_computation.16 | async-start | bytes 5308416 | tf_op jit(solution)/shard_map/reduce_scatter | solution.py:313
  816.6 1.4 copy-start
  816.6 418.0 %copy-start.2 = (f32[512,768]{1,0:T(8,128)S(1)}, f32[512,768]{1,0:T(8,128)}, u32[]{:S(2)}) copy-start(f32[512,768]{1,0:T(8,128)} %copy-done.1) | copy-start | bytes 4718596
  816.6 418.0 %copy-start.23 = (f32[512]{0:T(512)S(1)}, f32[512]{0:T(512)}, u32[]{:S(2)}) copy-start(f32[512]{0:T(512)} %copy-done.22) | copy-start | bytes 6148
  816.6 418.0 %copy-start.29 = (f32[768]{0:T(1024)S(1)}, f32[768]{0:T(1024)}, u32[]{:S(2)}) copy-start(f32[768]{0:T(1024)} %copy-done.28) | copy-start | bytes 9220
  816.6 418.0 %copy-start.33 = (f32[512]{0:T(512)S(1)}, f32[512]{0:T(512)}, u32[]{:S(2)}) copy-start(f32[512]{0:T(512)} %copy-done.32) | copy-start | bytes 6148
  816.6 418.0 %copy-start.36 = (f32[768]{0:T(1024)S(1)}, f32[768]{0:T(1024)}, u32[]{:S(2)}) copy-start(f32[768]{0:T(1024)} %copy-done.35) | copy-start | bytes 9220
  816.7 831.7 %reduce-scatter.11.cloned.1.call-start = ((), (), s32[]{:S(2)}) async-start(), calls=%async_computation.13 | async-start | bytes 3981312 | tf_op jit(solution)/shard_map/reduce_scatter | solution.py:295
  1240.1 65.2 %copy-start.25 = (f32[512]{0:T(512)S(1)}, f32[512]{0:T(512)}, u32[]{:S(2)}) copy-start(f32[512]{0:T(512)} %copy-done.24) | copy-start | bytes 6148
  1240.1 573.5 %reduce-scatter.9.cloned.1.call-start = ((), (), s32[]{:S(2)}) async-start(), calls=%async_computation.12 | async-start | bytes 10616832 | tf_op jit(solution)/shard_map/reduce_scatter | solution.py:286
  1305.3 1.4 copy-start.8
  1305.3 1.6 copy-start.12
  1305.3 1.6 copy-start.27
  1317.8 1.6 copy-start.13
  1317.8 1.7 copy-start.49
  1317.8 2.0 copy-start.34
  1317.8 2.0 copy-start.39
  1317.8 2.0 copy-start.40
  1317.9 495.8 %copy-start.6 = (f32[512,768]{1,0:T(8,128)S(1)}, f32[512,768]{1,0:T(8,128)}, u32[]{:S(2)}) copy-start(f32[512,768]{1,0:T(8,128)} %copy-done.3) | copy-start | bytes 4718596
  1317.9 563.0 %all-reduce.17.cloned.1.call-start = ((), (), s32[]{:S(2)}) async-start(), calls=%async_computation.18 | async-start | bytes 5898240 | tf_op jit(solution)/shard_map/psum | solution.py:321
  1880.9 6.4 copy-start.20
  1880.9 7.5 copy-start.19
  (4 other events, 3.9 us)
Sparse Core Ops, SparseCore 0:
  10.2 226.7 all-gather.8
  259.7 191.1 all-gather.18
  453.0 39.2 all-gather.10
  494.4 77.9 all-gather.12
  574.4 77.6 all-gather.14
  797.4 437.1 reduce-scatter.6
  1236.8 63.6 all-gather.16
  1304.5 63.5 reduce-scatter.12
  1372.3 94.5 reduce-scatter.14
  1470.4 95.2 reduce-scatter.16
  1569.3 79.0 reduce-scatter.10
  1651.8 161.7 reduce-scatter.8
  1816.3 64.5 all-reduce.16
